TPU v7x, 32 devices: a whole 2x2x4 slice. The times are simulated.
32 devices in a mesh: lon: 4 (over y, x), lat: 8 (over z, core).
Axes of the slice: x: 2, y: 2, z: 4, core: 2. Of those that a mesh axis runs over, the one named last changes fastest.
Arguments:
- state_adjoint: float32 [4, 4, 512, 1024], P(None, None, 'lat', 'lon'), may hold values from -6 to 6
- east_velocity: float32 [4, 512, 1024], P(None, 'lat', 'lon'), may hold values from -1.2 to 1.2
- north_velocity: float32 [4, 512, 1024], P(None, 'lat', 'lon'), may hold values from -1.2 to 1.2
- ocean_mask: int32 [4, 512, 1024], P(None, 'lat', 'lon'), may hold values 0 or 1
- partner: int32 [1024], P('lon'), may hold values from 0 to 1023, as said below
Outputs:
- sensitivity: float32 [4, 4, 512, 1024], P(None, None, 'lat', 'lon')
Inputs may be any that keep to these rules, and one draw needn't show every extreme that they name: partner[i] = (c - i) mod 1024 with one c for all columns, 1023 <= c <= 1278; hence partner[partner[i]] = i.
All inputs are finite; a program needn't handle non-finite values. No bound on the sum of `ocean_mask` on one device may be relied on, other than what follows from the above.
Results may differ from a plain program's by a relative error of at most 0.00002.
Values sent between devices are 32-bit elements; how exact they have to be, the bound alone decides.
No kernel may reach another device: no remote copies, remote signals or barrier semaphores. Data moves between devices by JAX's collectives and lax.ppermute only.
A program may use at most 64 MiB of HBM per device.

v0:
```python
import jax
import jax.numpy as jnp
from jax import lax
from jax.sharding import PartitionSpec as P

STEPS = 2


def shifted(shard, axis, by):
    count = lax.axis_size(axis)
    return lax.ppermute(shard, axis, [(i, (i + by) % count) for i in range(count)])


def shifted_2(shard, axis, by):
    count = lax.axis_size(axis)
    pairs = [(i, i + by) for i in range(count) if 0 <= i + by < count]
    return lax.ppermute(shard, axis, pairs)


def with_halo(block, sides, width, periodic):
    for axis, dim in sides:
        count = lax.axis_size(axis)
        forward = [(i, i + 1) for i in range(count - 1)]
        if periodic:
            forward.append((count - 1, 0))
        backward = [(target, source) for source, target in forward]
        low = lax.ppermute(
            lax.slice_in_dim(block, block.shape[dim] - width, None, axis=dim), axis, forward
        )
        high = lax.ppermute(lax.slice_in_dim(block, 0, width, axis=dim), axis, backward)
        block = jnp.concatenate([low, block, high], axis=dim)
    return block


def per_device(state_adjoint, east_velocity, north_velocity, ocean_mask, partner):
    wet_cells = ocean_mask.astype(jnp.float32)
    fold_signs = jnp.array([1.0, 1.0, -1.0, -1.0], dtype=jnp.float32).reshape(4, 1, 1)
    lat_place = lax.axis_index("lat")
    lat_count = lax.axis_size("lat")
    is_top = (lat_place == lat_count - 1).astype(jnp.float32)
    speed_west_edge = shifted(east_velocity[:, :, -1:], "lon", 1)
    speed_south_edge = shifted_2(north_velocity[:, -1:, :], "lat", 1)
    west_speed = jnp.concatenate([speed_west_edge, east_velocity[:, :, :-1]], axis=2)
    south_speed = jnp.concatenate([speed_south_edge, north_velocity[:, :-1, :]], axis=1)
    fold_weight = 1.0 + north_velocity[:, -1, :]
    current = state_adjoint
    for iteration in range(STEPS):
        masked = wet_cells * current
        lon_padded = with_halo(masked, (("lon", 3),), 1, True)
        lat_padded = with_halo(masked, (("lat", 2),), 1, False)
        west_rim = lon_padded[:, :, :, 0]
        east_rim = lon_padded[:, :, :, -1]
        south_rim = lat_padded[:, :, 0, :]
        north_rim = lat_padded[:, :, -1, :]
        east_adj = jnp.concatenate([masked[..., 1:], east_rim[..., None]], axis=3)
        west_adj = jnp.concatenate([west_rim[..., None], masked[..., :-1]], axis=3)
        north_adj = jnp.concatenate([masked[:, :, 1:, :], north_rim[:, :, None, :]], axis=2)
        south_adj = jnp.concatenate([south_rim[:, :, None, :], masked[:, :, :-1, :]], axis=2)
        transport = (
            0.5 * east_velocity * (east_adj - masked)
            + 0.5 * west_speed * (masked - west_adj)
            + 0.5 * north_velocity * (north_adj - masked)
            + 0.5 * south_speed * (masked - south_adj)
        )
        fold_flux = fold_weight * masked[:, :, -1, :]
        whole_row = lax.all_gather(fold_flux, "lon", axis=2, tiled=True)
        picked = jnp.take(whole_row, partner, axis=2)
        folded = 0.5 * fold_signs * picked
        total = masked + transport
        total = total.at[:, :, -1, :].add(is_top * folded)
        current = wet_cells * total
    return current


def solution(mesh):
    placed = (
        P(None, None, "lat", "lon"),
        P(None, "lat", "lon"),
        P(None, "lat", "lon"),
        P(None, "lat", "lon"),
        P("lon"),
    )
    return jax.shard_map(
        per_device,
        mesh=mesh,
        in_specs=placed,
        out_specs=P(None, None, "lat", "lon"),
        check_vma=False,
    )
```

profile of v0, /device:TPU:10, one launch (start us, length us, event | category | flops | bytes accessed | tf_op | source)
XLA Modules:
  0.0 109.1 jit_solution(16763126374377405692)
XLA Ops:
  0.0 0.8 broadcast_add_fusion
  0.8 1.9 %collective-permute-start.4 = (f32[4,1,256]{2,1,0:T(1,128)S(1)}, f32[4,1,256]{2,1,0:T(1,128)S(1)}, u32[]{:S(2)}, u32[]{:S(2)}) collective-permute-start(f32[4,1,256]{2,1,0:T(1,128)S(1)} %get-tuple-element.47), channel_id=1, source_target_pairs={{0,1},{1,2},{2,3},{3,4},{4,5},{5,6},{6,7},{8,9},{9,10},{10,11},{11... | collective-permute-start | bytes 12296 | tf_op jit(solution)/shard_map/ppermute | solution.py:17
  2.7 1.7 %slice.119 = f32[4,64,1]{2,1,0:T(8,128)} slice(f32[4,64,256]{2,1,0:T(8,128)} %param.13), slice={[0:4], [0:64], [255:256]} | slice | bytes 2048 | tf_op jit(solution)/shard_map/slice | solution.py:41
  4.3 1.5 %collective-permute-start.1 = (f32[4,64,1]{2,1,0:T(8,128)}, f32[4,64,1]{2,1,0:T(8,128)}, u32[]{:S(2)}, u32[]{:S(2)}) collective-permute-start(f32[4,64,1]{2,1,0:T(8,128)} %slice.119), channel_id=1, source_target_pairs={{0,8},{8,16},{16,24},{24,0},{1,9},{9,17},{17,25},{25,1},{2,10},{10... | collective-permute-start | bytes 3080 | tf_op jit(solution)/shard_map/ppermute | solution.py:11
  5.8 1.0 convert_element_type.6
  6.8 0.2 copy.78
  7.0 0.0 copy-start.8
  7.0 0.0 copy-start.4
  7.0 0.0 copy-start.5
  7.0 2.1 %copy_multiply_fusion = f32[4,4,64,256]{3,1,0,2:T(4,128)S(1)} fusion(f32[4,4,64,256]{3,2,1,0:T(8,128)} %param.12, f32[4,64,256]{2,0,1:T(4,128)S(1)} %copy.78), kind=kLoop, calls=%fused_computation.26 | loop fusion | flops 262144 | bytes 2359296 | tf_op jit(solution)/shard_map/mul | solution.py:48
  9.1 3.3 %collective-permute-start.5 = (f32[4,4,1,256]{3,1,0,2:T(4,128)S(1)}, f32[4,4,1,256]{3,1,0,2:T(4,128)S(1)}, u32[]{:S(2)}, u32[]{:S(2)}) collective-permute-start(f32[4,4,1,256]{3,1,0,2:T(4,128)S(1)} %get-tuple-element.38), channel_id=1, source_target_pairs={{0,1},{1,2},{2,3},{3,4},{4,5},{5,6},{6,7},{8,9},{9,10},{10,11},{11... | collective-permute-start | bytes 49160 | tf_op jit(solution)/shard_map/ppermute | solution.py:27
  12.4 2.3 %collective-permute-start.3 = (f32[4,4,1,256]{3,1,0,2:T(4,128)S(1)}, f32[4,4,1,256]{3,1,0,2:T(4,128)S(1)}, u32[]{:S(2)}, u32[]{:S(2)}) collective-permute-start(f32[4,4,1,256]{3,1,0,2:T(4,128)S(1)} %get-tuple-element.39), channel_id=1, source_target_pairs={{1,0},{2,1},{3,2},{4,3},{5,4},{6,5},{7,6},{9,8},{10,9},{11,10},{12... | collective-permute-start | bytes 49160 | tf_op jit(solution)/shard_map/ppermute | solution.py:30
  14.7 1.3 %fusion.26 = (f32[4,4,64,1]{3,1,0,2:T(4,128)}, f32[4,4,64,1]{3,1,0,2:T(4,128)}) fusion(f32[4,4,64,256]{3,1,0,2:T(4,128)S(1)} %copy_multiply_fusion), kind=kLoop, calls=%fused_computation.54 | loop fusion | bytes 16384 | tf_op jit(solution)/shard_map/slice | solution.py:28
  16.0 1.5 %collective-permute-start.2 = (f32[4,4,64,1]{3,1,0,2:T(4,128)}, f32[4,4,64,1]{3,1,0,2:T(4,128)}, u32[]{:S(2)}, u32[]{:S(2)}) collective-permute-start(f32[4,4,64,1]{3,1,0,2:T(4,128)} %get-tuple-element.42), channel_id=1, source_target_pairs={{0,8},{8,16},{16,24},{24,0},{1,9},{9,17},{17,25},{25,1},{2,10},{10... | collective-permute-start | bytes 12296 | tf_op jit(solution)/shard_map/ppermute | solution.py:27
  17.5 0.5 compare_and_fusion
  18.1 1.8 %fusion.25 = (f32[4,4,63,256]{3,1,0,2:T(4,128)}, f32[4,4,63,256]{3,1,0,2:T(4,128)}) fusion(f32[4,4,64,256]{3,1,0,2:T(4,128)S(1)} %copy_multiply_fusion), kind=kLoop, calls=%fused_computation.53 | loop fusion | bytes 4128768 | tf_op jit(solution)/shard_map/slice | solution.py:58
  19.9 1.7 %fusion.27 = (f32[4,4,64,255]{3,1,0,2:T(4,128)S(1)}, f32[4,4,64,255]{3,1,0,2:T(4,128)}) fusion(f32[4,4,64,256]{3,1,0,2:T(4,128)S(1)} %copy_multiply_fusion), kind=kLoop, calls=%fused_computation.55 | loop fusion | bytes 4177920 | tf_op jit(solution)/shard_map/slice | solution.py:56
  21.6 12.3 %all_gather.6 = f32[4,4,1024]{2,1,0:T(4,128)S(1)} all-gather(f32[4,4,256]{2,1,0:T(4,128)S(1)} %bitcast_multiply_fusion.3), channel_id=1, replica_groups=mesh['lon'=4,'lat'=8] {'lon'}, dimensions={2}, use_global_device_ids=true | all-gather | bytes 81920 | tf_op jit(solution)/shard_map/all_gather | solution.py:66
  33.9 0.9 copy.80
  34.8 0.9 copy.82
  35.7 1.7 %copy.84 = f32[4,4,1024]{1,0,2:T(4,128)} copy(f32[4,4,1024]{2,1,0:T(4,128)S(1)} %all_gather.6) | data formatting | bytes 131072 | tf_op jit(solution)/shard_map/all_gather | solution.py:66
  37.4 2.6 %gather_fusion = f32[256,4,4]{2,1,0:T(4,128)S(1)} fusion(f32[4,4,1024]{1,0,2:T(4,128)} %copy.84, s32[1024]{0:T(1024)S(1)} %pad_clamp_fusion), kind=kCustom, calls=%fused_computation.clone | custom fusion | bytes 33792 | tf_op jit(solution)/shard_map/jit(_take)/gather | solution.py:67
  40.0 0.2 copy.85
  40.2 0.4 collective-permute-start
  40.6 1.0 maximum_multiply_fusion
  41.6 0.2 copy.81
  41.9 0.2 copy.83
  42.1 12.2 %collective-permute-done = f32[4,4,64,1]{3,1,0,2:T(4,128)S(1)} collective-permute-done((f32[4,4,64,1]{3,1,0,2:T(4,128)}, f32[4,4,64,1]{3,1,0,2:T(4,128)S(1)}, u32[]{:S(2)}, u32[]{:S(2)}) %collective-permute-start) | collective-permute-done | bytes 4128 | tf_op jit(solution)/shard_map/ppermute | solution.py:30
  54.3 0.0 copy-start.6
  54.4 4.6 %fusion.4 = f32[4,4,64,256]{3,1,0,2:T(4,128)S(1)} fusion(f32[4,4,64,1]{3,1,0,2:T(4,128)S(1)} %collective-permute-done, f32[4,4,64,255]{3,1,0,2:T(4,128)} %get-tuple-element.45, f32[4,4,64,255]{3,1,0,2:T(4,128)S(1)} %get-tuple-element.44, f32[4,4,64,1]{3,1,0,2:T(4,128)} %collective-permute-done.2, f32[4,4,1,256]{3,1,0,2:T(4,128)S(1)} %collective-permute-done.3, ...), kind=kLoop, calls=%fused_computation.7 | loop fusion | flops 4456448 | bytes 7602176 | tf_op jit(solution)/shard_map/add | solution.py:69
  59.0 0.1 fusion.17
  59.1 0.3 multiply_multiply_fusion
  59.5 1.4 %fusion.22 = (f32[4,4,64,1]{3,1,0,2:T(4,128)}, f32[4,4,64,1]{3,1,0,2:T(4,128)}) fusion(f32[4,4,64,256]{3,1,0,2:T(4,128)S(1)} %multiply_multiply_fusion), kind=kLoop, calls=%fused_computation.50 | loop fusion | bytes 16384 | tf_op jit(solution)/shard_map/slice | solution.py:28
  60.8 1.8 %fusion.21 = (f32[4,4,63,256]{3,1,0,2:T(4,128)}, f32[4,4,63,256]{3,1,0,2:T(4,128)}) fusion(f32[4,4,64,256]{3,1,0,2:T(4,128)S(1)} %multiply_multiply_fusion), kind=kLoop, calls=%fused_computation.49 | loop fusion | bytes 4128768 | tf_op jit(solution)/shard_map/slice | solution.py:58
  62.6 0.7 fusion.23
  63.4 1.9 %collective-permute-start.9 = (f32[4,4,1,256]{3,1,0,2:T(4,128)S(1)}, f32[4,4,1,256]{3,1,0,2:T(4,128)S(1)}, u32[]{:S(2)}, u32[]{:S(2)}) collective-permute-start(f32[4,4,1,256]{3,1,0,2:T(4,128)S(1)} %get-tuple-element.30), channel_id=1, source_target_pairs={{0,1},{1,2},{2,3},{3,4},{4,5},{5,6},{6,7},{8,9},{9,10},{10,11},{11... | collective-permute-start | bytes 49160 | tf_op jit(solution)/shard_map/ppermute | solution.py:27
  65.3 3.6 %collective-permute-start.8 = (f32[4,4,1,256]{3,1,0,2:T(4,128)S(1)}, f32[4,4,1,256]{3,1,0,2:T(4,128)S(1)}, u32[]{:S(2)}, u32[]{:S(2)}) collective-permute-start(f32[4,4,1,256]{3,1,0,2:T(4,128)S(1)} %get-tuple-element.31), channel_id=1, source_target_pairs={{1,0},{2,1},{3,2},{4,3},{5,4},{6,5},{7,6},{9,8},{10,9},{11,10},{12... | collective-permute-start | bytes 49160 | tf_op jit(solution)/shard_map/ppermute | solution.py:30
  69.0 0.4 collective-permute-start.7
  69.4 1.7 %collective-permute-start.6 = (f32[4,4,64,1]{3,1,0,2:T(4,128)}, f32[4,4,64,1]{3,1,0,2:T(4,128)}, u32[]{:S(2)}, u32[]{:S(2)}) collective-permute-start(f32[4,4,64,1]{3,1,0,2:T(4,128)} %get-tuple-element.35), channel_id=1, source_target_pairs={{8,0},{16,8},{24,16},{0,24},{9,1},{17,9},{25,17},{1,25},{10,2},{18... | collective-permute-start | bytes 12296 | tf_op jit(solution)/shard_map/ppermute | solution.py:30
  71.0 25.6 %all_gather.7 = f32[4,4,1024]{2,1,0:T(4,128)S(1)} all-gather(f32[4,4,256]{2,1,0:T(4,128)S(1)} %bitcast_multiply_fusion.1), channel_id=1, replica_groups=mesh['lon'=4,'lat'=8] {'lon'}, dimensions={2}, use_global_device_ids=true | all-gather | bytes 81920 | tf_op jit(solution)/shard_map/all_gather | solution.py:66
  96.7 1.7 %copy.86 = f32[4,4,1024]{1,0,2:T(4,128)} copy(f32[4,4,1024]{2,1,0:T(4,128)S(1)} %all_gather.7) | data formatting | bytes 131072 | tf_op jit(solution)/shard_map/all_gather | solution.py:66
  98.4 3.4 %gather_fusion.1 = f32[256,4,4]{2,1,0:T(4,128)} fusion(f32[4,4,1024]{1,0,2:T(4,128)} %copy.86, s32[1024]{0:T(1024)S(1)} %pad_clamp_fusion), kind=kCustom, calls=%fused_computation.1.clone | custom fusion | bytes 33792 | tf_op jit(solution)/shard_map/jit(_take)/gather | solution.py:67
  101.7 1.2 %copy.87 = f32[256,4,4]{0,2,1:T(4,128)S(1)} copy(f32[256,4,4]{2,1,0:T(4,128)} %gather_fusion.1) | data formatting | bytes 32768 | tf_op jit(solution)/shard_map/jit(_take)/gather | solution.py:67
  103.0 0.0 collective-permute-done.9
  103.0 4.1 %fusion.12 = f32[4,4,64,256]{3,1,0,2:T(4,128)S(1)} fusion(f32[4,4,64,1]{3,1,0,2:T(4,128)} %collective-permute-done.6, f32[4,4,64,255]{3,1,0,2:T(4,128)S(1)} %get-tuple-element.37, f32[4,4,64,255]{3,1,0,2:T(4,128)S(1)} %get-tuple-element.36, f32[4,4,64,1]{3,1,0,2:T(4,128)} %collective-permute-done.7, f32[4,4,1,256]{3,1,0,2:T(4,128)S(1)} %collective-permute-done.8, ...), kind=kLoop, calls=%fused_computation.19 | loop fusion | flops 4718592 | bytes 7602176 | tf_op jit(solution)/shard_map/add | solution.py:69
  107.1 0.1 fusion.16
  107.2 0.3 broadcast_multiply_fusion
  107.5 1.6 %copy.88 = f32[4,4,64,256]{3,2,1,0:T(8,128)} copy(f32[4,4,64,256]{3,1,0,2:T(4,128)S(1)} %broadcast_multiply_fusion) | data formatting | bytes 2097152 | tf_op jit(solution)/shard_map/mul | solution.py:71
  (32 shorter events, 0.2 us)
Async XLA Ops:
  0.8 41.1 %collective-permute-start.4 = (f32[4,1,256]{2,1,0:T(1,128)S(1)}, f32[4,1,256]{2,1,0:T(1,128)S(1)}, u32[]{:S(2)}, u32[]{:S(2)}) collective-permute-start(f32[4,1,256]{2,1,0:T(1,128)S(1)} %get-tuple-element.47), channel_id=1, source_target_pairs={{0,1},{1,2},{2,3},{3,4},{4,5},{5,6},{6,7},{8,9},{9,10},{10,11},{11... | collective-permute-start | bytes 12296 | tf_op jit(solution)/shard_map/ppermute | solution.py:17
  4.3 35.8 %collective-permute-start.1 = (f32[4,64,1]{2,1,0:T(8,128)}, f32[4,64,1]{2,1,0:T(8,128)}, u32[]{:S(2)}, u32[]{:S(2)}) collective-permute-start(f32[4,64,1]{2,1,0:T(8,128)} %slice.119), channel_id=1, source_target_pairs={{0,8},{8,16},{16,24},{24,0},{1,9},{9,17},{17,25},{25,1},{2,10},{10... | collective-permute-start | bytes 3080 | tf_op jit(solution)/shard_map/ppermute | solution.py:11
  7.0 10.5 %copy-start.8 = (s32[256]{0:T(256)S(1)}, s32[256]{0:T(256)}, u32[]{:S(2)}) copy-start(s32[256]{0:T(256)} %param.16) | copy-start | bytes 3076
  7.0 11.0 %copy-start.4 = (f32[4,64,256]{2,1,0:T(8,128)S(1)}, f32[4,64,256]{2,1,0:T(8,128)}, u32[]{:S(2)}) copy-start(f32[4,64,256]{2,1,0:T(8,128)} %param.13) | copy-start | bytes 786436
  7.0 11.0 %copy-start.5 = (f32[4,64,256]{2,1,0:T(8,128)S(1)}, f32[4,64,256]{2,1,0:T(8,128)}, u32[]{:S(2)}) copy-start(f32[4,64,256]{2,1,0:T(8,128)} %param.14) | copy-start | bytes 786436
  9.1 45.2 %collective-permute-start.5 = (f32[4,4,1,256]{3,1,0,2:T(4,128)S(1)}, f32[4,4,1,256]{3,1,0,2:T(4,128)S(1)}, u32[]{:S(2)}, u32[]{:S(2)}) collective-permute-start(f32[4,4,1,256]{3,1,0,2:T(4,128)S(1)} %get-tuple-element.38), channel_id=1, source_target_pairs={{0,1},{1,2},{2,3},{3,4},{4,5},{5,6},{6,7},{8,9},{9,10},{10,11},{11... | collective-permute-start | bytes 49160 | tf_op jit(solution)/shard_map/ppermute | solution.py:27
  12.4 41.9 %collective-permute-start.3 = (f32[4,4,1,256]{3,1,0,2:T(4,128)S(1)}, f32[4,4,1,256]{3,1,0,2:T(4,128)S(1)}, u32[]{:S(2)}, u32[]{:S(2)}) collective-permute-start(f32[4,4,1,256]{3,1,0,2:T(4,128)S(1)} %get-tuple-element.39), channel_id=1, source_target_pairs={{1,0},{2,1},{3,2},{4,3},{5,4},{6,5},{7,6},{9,8},{10,9},{11,10},{12... | collective-permute-start | bytes 49160 | tf_op jit(solution)/shard_map/ppermute | solution.py:30
  16.0 26.0 %collective-permute-start.2 = (f32[4,4,64,1]{3,1,0,2:T(4,128)}, f32[4,4,64,1]{3,1,0,2:T(4,128)}, u32[]{:S(2)}, u32[]{:S(2)}) collective-permute-start(f32[4,4,64,1]{3,1,0,2:T(4,128)} %get-tuple-element.42), channel_id=1, source_target_pairs={{0,8},{8,16},{16,24},{24,0},{1,9},{9,17},{17,25},{25,1},{2,10},{10... | collective-permute-start | bytes 12296 | tf_op jit(solution)/shard_map/ppermute | solution.py:27
  35.7 18.7 %copy-start = (f32[4,4,64,256]{3,2,1,0:T(8,128)S(1)}, f32[4,4,64,256]{3,2,1,0:T(8,128)}, u32[]{:S(2)}) copy-start(f32[4,4,64,256]{3,2,1,0:T(8,128)} %param.12) | copy-start | bytes 3145732
  40.2 14.2 %copy-start.1 = (f32[4,64,256]{2,0,1:T(4,128)S(1)}, f32[4,64,256]{2,0,1:T(4,128)}, u32[]{:S(2)}) copy-start(f32[4,64,256]{2,0,1:T(4,128)} %copy.82) | copy-start | bytes 786436
  40.2 14.1 %collective-permute-start = (f32[4,4,64,1]{3,1,0,2:T(4,128)}, f32[4,4,64,1]{3,1,0,2:T(4,128)S(1)}, u32[]{:S(2)}, u32[]{:S(2)}) collective-permute-start(f32[4,4,64,1]{3,1,0,2:T(4,128)} %get-tuple-element.43), channel_id=1, source_target_pairs={{8,0},{16,8},{24,16},{0,24},{9,1},{17,9},{25,17},{1,25},{10,2},{18... | collective-permute-start | bytes 12296 | tf_op jit(solution)/shard_map/ppermute | solution.py:30
  41.8 17.2 %copy-start.2 = (f32[4,64,256]{2,0,1:T(4,128)}, f32[4,64,256]{2,0,1:T(4,128)S(1)}, u32[]{:S(2)}) copy-start(f32[4,64,256]{2,0,1:T(4,128)S(1)} %copy.81) | copy-start | bytes 786436
  42.1 17.0 %copy-start.3 = (f32[4,64,256]{2,0,1:T(4,128)}, f32[4,64,256]{2,0,1:T(4,128)S(1)}, u32[]{:S(2)}) copy-start(f32[4,64,256]{2,0,1:T(4,128)S(1)} %copy.83) | copy-start | bytes 786436
  54.3 4.7 %copy-start.6 = (f32[4]{0:T(128)S(1)}, f32[4]{0:T(128)}, u32[]{:S(2)}) copy-start(f32[4]{0:T(128)} %constant.73) | copy-start | bytes 52
  54.4 4.7 %copy-start.7 = (pred[256]{0:T(512)(128)(4,1)S(1)}, pred[256]{0:T(512)(128)(4,1)}, u32[]{:S(2)}) copy-start(pred[256]{0:T(512)(128)(4,1)} %compare_and_fusion) | copy-start | bytes 772
  63.4 39.6 %collective-permute-start.9 = (f32[4,4,1,256]{3,1,0,2:T(4,128)S(1)}, f32[4,4,1,256]{3,1,0,2:T(4,128)S(1)}, u32[]{:S(2)}, u32[]{:S(2)}) collective-permute-start(f32[4,4,1,256]{3,1,0,2:T(4,128)S(1)} %get-tuple-element.30), channel_id=1, source_target_pairs={{0,1},{1,2},{2,3},{3,4},{4,5},{5,6},{6,7},{8,9},{9,10},{10,11},{11... | collective-permute-start | bytes 49160 | tf_op jit(solution)/shard_map/ppermute | solution.py:27
  65.3 37.7 %collective-permute-start.8 = (f32[4,4,1,256]{3,1,0,2:T(4,128)S(1)}, f32[4,4,1,256]{3,1,0,2:T(4,128)S(1)}, u32[]{:S(2)}, u32[]{:S(2)}) collective-permute-start(f32[4,4,1,256]{3,1,0,2:T(4,128)S(1)} %get-tuple-element.31), channel_id=1, source_target_pairs={{1,0},{2,1},{3,2},{4,3},{5,4},{6,5},{7,6},{9,8},{10,9},{11,10},{12... | collective-permute-start | bytes 49160 | tf_op jit(solution)/shard_map/ppermute | solution.py:30
  69.0 34.0 %collective-permute-start.7 = (f32[4,4,64,1]{3,1,0,2:T(4,128)}, f32[4,4,64,1]{3,1,0,2:T(4,128)}, u32[]{:S(2)}, u32[]{:S(2)}) collective-permute-start(f32[4,4,64,1]{3,1,0,2:T(4,128)} %get-tuple-element.34), channel_id=1, source_target_pairs={{0,8},{8,16},{16,24},{24,0},{1,9},{9,17},{17,25},{25,1},{2,10},{10... | collective-permute-start | bytes 12296 | tf_op jit(solution)/shard_map/ppermute | solution.py:27
  69.4 33.6 %collective-permute-start.6 = (f32[4,4,64,1]{3,1,0,2:T(4,128)}, f32[4,4,64,1]{3,1,0,2:T(4,128)}, u32[]{:S(2)}, u32[]{:S(2)}) collective-permute-start(f32[4,4,64,1]{3,1,0,2:T(4,128)} %get-tuple-element.35), channel_id=1, source_target_pairs={{8,0},{16,8},{24,16},{0,24},{9,1},{17,9},{25,17},{1,25},{10,2},{18... | collective-permute-start | bytes 12296 | tf_op jit(solution)/shard_map/ppermute | solution.py:30
where the time goes:
time: 110 us; the launch traced here: 109 us
  blocking collectives  37.9 us (34%)
  local copies, waits for them, and re-layouts  25.1 us (23%)
  starting transfers between devices  18.5 us (17%)
  other arithmetic  14.9 us (14%)
  waiting for transfers between devices  12.3 us (11%)
    all_gather x2, blocking collectives, per_device(): whole_row = lax.all_gather(fold_flux, 'lon', axis=2, tiled=True)  37.9 us
    ppermute x4, waiting for transfers between devices, with_halo(): lax.ppermute(lax.slice_in_dim(block, 0, width, axis=dim), axis, backward)  12.2 us
    add x2, other arithmetic, per_device(): total = masked + transport  8.75 us
    ppermute x4, starting transfers between devices, with_halo(): lax.ppermute(lax.slice_in_dim(block, 0, width, axis=dim), axis, backward)  8 us
    gather x4, local copies, waits for them, and re-layouts, per_device(): picked = jnp.take(whole_row, partner, axis=2)  7.4 us
    ppermute x4, starting transfers between devices, with_halo(): lax.ppermute(lax.slice_in_dim(block, block.shape[dim] - width, None, axis...  7.11 us
    slice x2, local copies, waits for them, and re-layouts, per_device(): masked[:, :, :-1, :]  3.65 us
    all_gather x2, local copies, waits for them, and re-layouts, per_device(): whole_row = lax.all_gather(fold_flux, 'lon', axis=2, tiled=True)  3.41 us
  transfers between devices with their start and end apart: 10, of which 1 were waited for; matrix products, arithmetic and copies ran while one was open for 22% of the time, Pallas kernels for 0%

commit v1 on v0

--- a/solution.py
+++ b/solution.py
@@ -4,6 +4,24 @@
 from jax.sharding import PartitionSpec as P
 
 STEPS = 2
+
+
+def joined_along(pieces, dim):
+    shape = list(pieces.shape[1:])
+    shape[dim] *= pieces.shape[0]
+    return jnp.moveaxis(pieces, 0, dim).reshape(shape)
+
+
+def grow_blocks(array, axis):
+    size = lax.axis_size(axis)
+    blocks = array[None]
+    for level in range(size.bit_length() - 1):
+        bit = 1 << level
+        other = lax.ppermute(blocks, axis, [(i, i ^ bit) for i in range(size)])
+        both = jnp.stack([blocks, other])
+        upper = lax.axis_index(axis) >> level & 1
+        blocks = jnp.where(upper == 0, both, both[::-1]).reshape(-1, *array.shape)
+    return blocks
 
 
 def shifted(shard, axis, by):
@@ -63,7 +81,7 @@
             + 0.5 * south_speed * (masked - south_adj)
         )
         fold_flux = fold_weight * masked[:, :, -1, :]
-        whole_row = lax.all_gather(fold_flux, "lon", axis=2, tiled=True)
+        whole_row = joined_along(grow_blocks(fold_flux, "lon"), 2)
         picked = jnp.take(whole_row, partner, axis=2)
         folded = 0.5 * fold_signs * picked
         total = masked + transport

time: 110 us -> 102 us (0.927)
  blocking collectives: 37.9 us -> 0 us
  waiting for transfers between devices: 12.3 us -> 43.5 us
  local copies, waits for them, and re-layouts: 25.1 us -> 19.7 us
  starting transfers between devices: 18.5 us -> 23.1 us
    all_gather x2 -> x0, blocking collectives: 37.9 us -> none  [per_device(): whole_row = lax.all_gather(fold_flux, 'lon', axis=2, tiled=True)]
    ppermute x4, waiting for transfers between devices: 0.01 us -> 21.1 us  [with_halo(): lax.ppermute(lax.slice_in_dim(block, block.shape[dim] - width, None, axis...]
    ppermute x4, waiting for transfers between devices: 12.2 us -> 22.4 us  [with_halo(): lax.ppermute(lax.slice_in_dim(block, 0, width, axis=dim), axis, backward)]
    ppermute x0 -> x4, starting transfers between devices: none -> 4.29 us  [grow_blocks(): other = lax.ppermute(blocks, axis, [(i, i ^ bit) for i in range(size)])]
    all_gather x2 -> x0, local copies, waits for them, and re-layouts: 3.41 us -> none  [per_device(): whole_row = lax.all_gather(fold_flux, 'lon', axis=2, tiled=True)]
    reshape x0 -> x2, local copies, waits for them, and re-layouts: none -> 2.63 us  [joined_along(): return jnp.moveaxis(pieces, 0, dim).reshape(shape)]
    add x2, other arithmetic: 8.75 us -> 7.06 us  [per_device(): total = masked + transport]
    gather x4, local copies, waits for them, and re-layouts: 7.4 us -> 5.78 us  [per_device(): picked = jnp.take(whole_row, partner, axis=2)]
  transfers between devices with their start and end apart: 10 -> 14, of which waited for: 1 -> 4; matrix products, arithmetic and copies ran while one was open for 22% -> 21% of each run, Pallas kernels for 0% -> 0%
where the time goes in v1:
time: 102 us; the launch traced here: 101 us
  waiting for transfers between devices  43.5 us (43%)
  starting transfers between devices  23.1 us (23%)
  local copies, waits for them, and re-layouts  19.7 us (19%)
  other arithmetic  14.4 us (14%)
    ppermute x4, waiting for transfers between devices, with_halo(): lax.ppermute(lax.slice_in_dim(block, 0, width, axis=dim), axis, backward)  22.4 us
    ppermute x4, waiting for transfers between devices, with_halo(): lax.ppermute(lax.slice_in_dim(block, block.shape[dim] - width, None, axis...  21.1 us
    ppermute x4, starting transfers between devices, with_halo(): lax.ppermute(lax.slice_in_dim(block, block.shape[dim] - width, None, axis...  7.91 us
    ppermute x4, starting transfers between devices, with_halo(): lax.ppermute(lax.slice_in_dim(block, 0, width, axis=dim), axis, backward)  7.4 us
    add x2, other arithmetic, per_device(): total = masked + transport  7.06 us
    gather x4, local copies, waits for them, and re-layouts, per_device(): picked = jnp.take(whole_row, partner, axis=2)  5.78 us
    ppermute x4, starting transfers between devices, grow_blocks(): other = lax.ppermute(blocks, axis, [(i, i ^ bit) for i in range(size)])  4.29 us
    reshape x2, local copies, waits for them, and re-layouts, joined_along(): return jnp.moveaxis(pieces, 0, dim).reshape(shape)  2.63 us
  transfers between devices with their start and end apart: 14, of which 4 were waited for; matrix products, arithmetic and copies ran while one was open for 21% of the time, Pallas kernels for 0%

profile of v1, /device:TPU:10, one launch (start us, length us, event | category | flops | bytes accessed | tf_op | source)
XLA Modules:
  0.0 101.3 jit_solution(9739158607010157350)
XLA Ops:
  0.0 0.8 broadcast_add_fusion
  0.8 2.1 %collective-permute-start.4 = (f32[4,1,256]{2,1,0:T(1,128)S(1)}, f32[4,1,256]{2,1,0:T(1,128)S(1)}, u32[]{:S(2)}, u32[]{:S(2)}) collective-permute-start(f32[4,1,256]{2,1,0:T(1,128)S(1)} %get-tuple-element.47), channel_id=1, source_target_pairs={{0,1},{1,2},{2,3},{3,4},{4,5},{5,6},{6,7},{8,9},{9,10},{10,11},{11... | collective-permute-start | bytes 12296 | tf_op jit(solution)/shard_map/ppermute | solution.py:35
  2.9 1.7 %slice.119 = f32[4,64,1]{2,1,0:T(8,128)} slice(f32[4,64,256]{2,1,0:T(8,128)} %param.13), slice={[0:4], [0:64], [255:256]} | slice | bytes 2048 | tf_op jit(solution)/shard_map/slice | solution.py:59
  4.5 1.5 %collective-permute-start.1 = (f32[4,64,1]{2,1,0:T(8,128)}, f32[4,64,1]{2,1,0:T(8,128)S(1)}, u32[]{:S(2)}, u32[]{:S(2)}) collective-permute-start(f32[4,64,1]{2,1,0:T(8,128)} %slice.119), channel_id=1, source_target_pairs={{0,8},{8,16},{16,24},{24,0},{1,9},{9,17},{17,25},{25,1},{2,10},{10... | collective-permute-start | bytes 3080 | tf_op jit(solution)/shard_map/ppermute | solution.py:29
  6.0 1.0 convert_element_type.6
  7.0 0.2 copy.101
  7.2 2.0 %copy_multiply_fusion = f32[4,4,64,256]{3,1,0,2:T(4,128)S(1)} fusion(f32[4,4,64,256]{3,2,1,0:T(8,128)} %param.12, f32[4,64,256]{2,0,1:T(4,128)S(1)} %copy.101), kind=kLoop, calls=%fused_computation.26 | loop fusion | flops 262144 | bytes 2359296 | tf_op jit(solution)/shard_map/mul | solution.py:66
  9.2 0.6 bitcast_multiply_fusion.4
  9.8 0.5 collective-permute-start.6
  10.3 0.6 fusion.28
  11.0 3.0 %collective-permute-start.5 = (f32[4,4,1,256]{3,1,0,2:T(4,128)}, f32[4,4,1,256]{3,1,0,2:T(4,128)}, u32[]{:S(2)}, u32[]{:S(2)}) collective-permute-start(f32[4,4,1,256]{3,1,0,2:T(4,128)} %get-tuple-element.38), channel_id=1, source_target_pairs={{0,1},{1,2},{2,3},{3,4},{4,5},{5,6},{6,7},{8,9},{9,10},{10,11},{11... | collective-permute-start | bytes 49160 | tf_op jit(solution)/shard_map/ppermute | solution.py:45
  14.0 2.5 %collective-permute-start.3 = (f32[4,4,1,256]{3,1,0,2:T(4,128)}, f32[4,4,1,256]{3,1,0,2:T(4,128)}, u32[]{:S(2)}, u32[]{:S(2)}) collective-permute-start(f32[4,4,1,256]{3,1,0,2:T(4,128)} %get-tuple-element.39), channel_id=1, source_target_pairs={{1,0},{2,1},{3,2},{4,3},{5,4},{6,5},{7,6},{9,8},{10,9},{11,10},{12... | collective-permute-start | bytes 49160 | tf_op jit(solution)/shard_map/ppermute | solution.py:48
  16.5 0.5 compare_and_fusion
  17.2 0.6 bitcast_multiply_fusion.5
  17.8 1.3 %fusion.30 = (f32[4,4,64,1]{3,1,0,2:T(4,128)}, f32[4,4,64,1]{3,1,0,2:T(4,128)}) fusion(f32[4,4,64,256]{3,1,0,2:T(4,128)S(1)} %copy_multiply_fusion), kind=kLoop, calls=%fused_computation.68 | loop fusion | bytes 16384 | tf_op jit(solution)/shard_map/slice | solution.py:46
  19.1 1.9 %fusion.29 = (f32[4,4,63,256]{3,1,0,2:T(4,128)}, f32[4,4,63,256]{3,1,0,2:T(4,128)}) fusion(f32[4,4,64,256]{3,1,0,2:T(4,128)S(1)} %copy_multiply_fusion), kind=kLoop, calls=%fused_computation.67 | loop fusion | bytes 4128768 | tf_op jit(solution)/shard_map/slice | solution.py:76
  21.0 1.7 %fusion.31 = (f32[4,4,64,255]{3,1,0,2:T(4,128)S(1)}, f32[4,4,64,255]{3,1,0,2:T(4,128)}) fusion(f32[4,4,64,256]{3,1,0,2:T(4,128)S(1)} %copy_multiply_fusion), kind=kLoop, calls=%fused_computation.69 | loop fusion | bytes 4177920 | tf_op jit(solution)/shard_map/slice | solution.py:74
  22.7 0.2 copy.103
  22.9 0.2 copy.105
  23.1 1.5 %collective-permute-start.2 = (f32[4,4,64,1]{3,1,0,2:T(4,128)}, f32[4,4,64,1]{3,1,0,2:T(4,128)S(1)}, u32[]{:S(2)}, u32[]{:S(2)}) collective-permute-start(f32[4,4,64,1]{3,1,0,2:T(4,128)} %get-tuple-element.42), channel_id=1, source_target_pairs={{0,8},{8,16},{16,24},{24,0},{1,9},{9,17},{17,25},{25,1},{2,10},{10... | collective-permute-start | bytes 12296 | tf_op jit(solution)/shard_map/ppermute | solution.py:45
  24.7 0.2 copy.104
  24.9 0.6 collective-permute-start
  25.8 0.8 pad_maximum_fusion.2
  26.6 1.6 %collective-permute-start.7 = (f32[2,4,4,256]{3,2,1,0:T(4,128)S(1)}, f32[2,4,4,256]{3,2,1,0:T(4,128)S(1)}, u32[]{:S(2)}, u32[]{:S(2)}) collective-permute-start(f32[2,4,4,256]{3,2,1,0:T(4,128)S(1)} %get-tuple-element.51), channel_id=1, source_target_pairs={{0,16},{8,24},{16,0},{24,8},{1,17},{9,25},{17,1},{25,9},{2,18},{10... | collective-permute-start | bytes 98312 | tf_op jit(solution)/shard_map/ppermute | solution.py:20
  28.2 10.0 %collective-permute-done.2 = f32[4,4,64,1]{3,1,0,2:T(4,128)S(1)} collective-permute-done((f32[4,4,64,1]{3,1,0,2:T(4,128)}, f32[4,4,64,1]{3,1,0,2:T(4,128)S(1)}, u32[]{:S(2)}, u32[]{:S(2)}) %collective-permute-start.2) | collective-permute-done | bytes 4128 | tf_op jit(solution)/shard_map/ppermute | solution.py:45
  38.1 11.2 %collective-permute-done = f32[4,4,64,1]{3,1,0,2:T(4,128)S(1)} collective-permute-done((f32[4,4,64,1]{3,1,0,2:T(4,128)}, f32[4,4,64,1]{3,1,0,2:T(4,128)S(1)}, u32[]{:S(2)}, u32[]{:S(2)}) %collective-permute-start) | collective-permute-done | bytes 4128 | tf_op jit(solution)/shard_map/ppermute | solution.py:48
  49.3 4.3 %fusion.4 = f32[4,4,64,256]{3,1,0,2:T(4,128)S(1)} fusion(f32[4,4,64,1]{3,1,0,2:T(4,128)S(1)} %collective-permute-done, f32[4,4,64,255]{3,1,0,2:T(4,128)S(1)} %copy-done.1, f32[4,4,64,255]{3,1,0,2:T(4,128)S(1)} %get-tuple-element.44, f32[4,4,64,1]{3,1,0,2:T(4,128)S(1)} %collective-permute-done.2, f32[4,4,1,256]{3,1,0,2:T(4,128)} %collective-permute-done.3, ...), kind=kLoop, calls=%fused_computation.7 | loop fusion | flops 4456448 | bytes 7602176 | tf_op jit(solution)/shard_map/add | solution.py:87
  53.8 1.8 %copy.114 = f32[4,4,4,256]{1,0,3,2:T(4,128)} copy(f32[4,4,4,256]{3,1,0,2:T(4,128)S(1)} %bitcast.56) | data formatting | bytes 131072 | tf_op jit(solution)/shard_map/reshape | solution.py:12
  55.6 2.6 %gather_fusion = f32[256,4,4]{2,1,0:T(4,128)S(1)} fusion(f32[4,4,1024]{1,0,2:T(4,128)} %bitcast.52, s32[1024]{0:T(1024)S(1)} %pad_clamp_fusion), kind=kCustom, calls=%fused_computation.clone | custom fusion | bytes 33792 | tf_op jit(solution)/shard_map/jit(_take)/gather | solution.py:85
  58.2 0.2 copy.109
  58.5 0.3 multiply_multiply_fusion
  58.8 0.3 fusion.26
  59.2 0.5 fusion.25
  59.7 0.7 fusion.27
  60.4 0.6 collective-permute-start.12
  61.0 1.9 %collective-permute-start.11 = (f32[4,4,1,256]{3,1,0,2:T(4,128)S(1)}, f32[4,4,1,256]{3,1,0,2:T(4,128)S(1)}, u32[]{:S(2)}, u32[]{:S(2)}) collective-permute-start(f32[4,4,1,256]{3,1,0,2:T(4,128)S(1)} %get-tuple-element.30), channel_id=1, source_target_pairs={{0,1},{1,2},{2,3},{3,4},{4,5},{5,6},{6,7},{8,9},{9,10},{10,11},{11... | collective-permute-start | bytes 49160 | tf_op jit(solution)/shard_map/ppermute | solution.py:45
  63.0 3.6 %collective-permute-start.10 = (f32[4,4,1,256]{3,1,0,2:T(4,128)S(1)}, f32[4,4,1,256]{3,1,0,2:T(4,128)S(1)}, u32[]{:S(2)}, u32[]{:S(2)}) collective-permute-start(f32[4,4,1,256]{3,1,0,2:T(4,128)S(1)} %get-tuple-element.31), channel_id=1, source_target_pairs={{1,0},{2,1},{3,2},{4,3},{5,4},{6,5},{7,6},{9,8},{10,9},{11,10},{12... | collective-permute-start | bytes 49160 | tf_op jit(solution)/shard_map/ppermute | solution.py:48
  66.6 1.5 %collective-permute-start.9 = (f32[4,4,64,1]{3,1,0,2:T(4,128)S(1)}, f32[4,4,64,1]{3,1,0,2:T(4,128)S(1)}, u32[]{:S(2)}, u32[]{:S(2)}) collective-permute-start(f32[4,4,64,1]{3,1,0,2:T(4,128)S(1)} %get-tuple-element.34), channel_id=1, source_target_pairs={{0,8},{8,16},{16,24},{24,0},{1,9},{9,17},{17,25},{25,1},{2,10},{10... | collective-permute-start | bytes 12296 | tf_op jit(solution)/shard_map/ppermute | solution.py:45
  68.1 0.6 collective-permute-start.8
  68.7 1.6 %collective-permute-start.13 = (f32[2,4,4,256]{3,2,1,0:T(4,128)S(1)}, f32[2,4,4,256]{3,2,1,0:T(4,128)S(1)}, u32[]{:S(2)}, u32[]{:S(2)}) collective-permute-start(f32[2,4,4,256]{3,2,1,0:T(4,128)S(1)} %get-tuple-element.49), channel_id=1, source_target_pairs={{0,16},{8,24},{16,0},{24,8},{1,17},{9,25},{17,1},{25,9},{2,18},{10... | collective-permute-start | bytes 98312 | tf_op jit(solution)/shard_map/ppermute | solution.py:20
  70.3 11.1 %collective-permute-done.9 = f32[4,4,64,1]{3,1,0,2:T(4,128)S(1)} collective-permute-done((f32[4,4,64,1]{3,1,0,2:T(4,128)S(1)}, f32[4,4,64,1]{3,1,0,2:T(4,128)S(1)}, u32[]{:S(2)}, u32[]{:S(2)}) %collective-permute-start.9) | collective-permute-done | bytes 4128 | tf_op jit(solution)/shard_map/ppermute | solution.py:45
  81.5 11.2 %collective-permute-done.8 = f32[4,4,64,1]{3,1,0,2:T(4,128)S(1)} collective-permute-done((f32[4,4,64,1]{3,1,0,2:T(4,128)S(1)}, f32[4,4,64,1]{3,1,0,2:T(4,128)S(1)}, u32[]{:S(2)}, u32[]{:S(2)}) %collective-permute-start.8) | collective-permute-done | bytes 4128 | tf_op jit(solution)/shard_map/ppermute | solution.py:48
  92.7 2.7 %fusion.12 = f32[4,4,64,256]{3,1,0,2:T(4,128)S(1)} fusion(f32[4,4,64,1]{3,1,0,2:T(4,128)S(1)} %collective-permute-done.8, f32[4,4,64,255]{3,1,0,2:T(4,128)S(1)} %get-tuple-element.37, f32[4,4,64,255]{3,1,0,2:T(4,128)S(1)} %get-tuple-element.36, f32[4,4,64,1]{3,1,0,2:T(4,128)S(1)} %collective-permute-done.9, f32[4,4,1,256]{3,1,0,2:T(4,128)S(1)} %collective-permute-done.10, ...), kind=kLoop, calls=%fused_computation.19 | loop fusion | flops 4718592 | bytes 7602176 | tf_op jit(solution)/shard_map/add | solution.py:87
  95.5 0.9 copy.115
  96.3 1.8 %gather_fusion.1 = f32[256,4,4]{2,1,0:T(4,128)} fusion(f32[4,4,1024]{1,0,2:T(4,128)S(1)} %bitcast.51, s32[1024]{0:T(1024)S(1)} %pad_clamp_fusion), kind=kCustom, calls=%fused_computation.1.clone | custom fusion | bytes 33792 | tf_op jit(solution)/shard_map/jit(_take)/gather | solution.py:85
  98.1 1.2 %copy.112 = f32[256,4,4]{0,2,1:T(4,128)S(1)} copy(f32[256,4,4]{2,1,0:T(4,128)} %gather_fusion.1) | data formatting | bytes 32768 | tf_op jit(solution)/shard_map/jit(_take)/gather | solution.py:85
  99.4 0.3 broadcast_multiply_fusion
  99.7 1.6 %copy.113 = f32[4,4,64,256]{3,2,1,0:T(8,128)} copy(f32[4,4,64,256]{3,1,0,2:T(4,128)S(1)} %broadcast_multiply_fusion) | data formatting | bytes 2097152 | tf_op jit(solution)/shard_map/mul | solution.py:89
  (62 shorter events, 0.8 us)
Async XLA Ops:
  0.0 17.1 %copy-start.10 = (f32[4,64,256]{2,1,0:T(8,128)S(1)}, f32[4,64,256]{2,1,0:T(8,128)}, u32[]{:S(2)}) copy-start(f32[4,64,256]{2,1,0:T(8,128)} %param.13) | copy-start | bytes 786436
  0.0 16.5 %copy-start.15 = (s32[256]{0:T(256)S(1)}, s32[256]{0:T(256)}, u32[]{:S(2)}) copy-start(s32[256]{0:T(256)} %param.16) | copy-start | bytes 3076
  0.8 16.3 %copy-start.11 = (f32[4,64,256]{2,1,0:T(8,128)S(1)}, f32[4,64,256]{2,1,0:T(8,128)}, u32[]{:S(2)}) copy-start(f32[4,64,256]{2,1,0:T(8,128)} %param.14) | copy-start | bytes 786436
  0.8 24.1 %collective-permute-start.4 = (f32[4,1,256]{2,1,0:T(1,128)S(1)}, f32[4,1,256]{2,1,0:T(1,128)S(1)}, u32[]{:S(2)}, u32[]{:S(2)}) collective-permute-start(f32[4,1,256]{2,1,0:T(1,128)S(1)} %get-tuple-element.47), channel_id=1, source_target_pairs={{0,1},{1,2},{2,3},{3,4},{4,5},{5,6},{6,7},{8,9},{9,10},{10,11},{11... | collective-permute-start | bytes 12296 | tf_op jit(solution)/shard_map/ppermute | solution.py:35
  4.5 18.5 %collective-permute-start.1 = (f32[4,64,1]{2,1,0:T(8,128)}, f32[4,64,1]{2,1,0:T(8,128)S(1)}, u32[]{:S(2)}, u32[]{:S(2)}) collective-permute-start(f32[4,64,1]{2,1,0:T(8,128)} %slice.119), channel_id=1, source_target_pairs={{0,8},{8,16},{16,24},{24,0},{1,9},{9,17},{17,25},{25,1},{2,10},{10... | collective-permute-start | bytes 3080 | tf_op jit(solution)/shard_map/ppermute | solution.py:29
  9.8 16.0 %collective-permute-start.6 = (f32[1,4,4,256]{3,2,1,0:T(4,128)}, f32[1,4,4,256]{3,2,1,0:T(4,128)}, u32[]{:S(2)}, u32[]{:S(2)}) collective-permute-start(f32[1,4,4,256]{3,2,1,0:T(4,128)} %bitcast_multiply_fusion.4), channel_id=1, source_target_pairs={{0,8},{8,0},{16,24},{24,16},{1,9},{9,1},{17,25},{25,17},{2,10},{10... | collective-permute-start | bytes 49160 | tf_op jit(solution)/shard_map/ppermute | solution.py:20
  11.0 38.4 %collective-permute-start.5 = (f32[4,4,1,256]{3,1,0,2:T(4,128)}, f32[4,4,1,256]{3,1,0,2:T(4,128)}, u32[]{:S(2)}, u32[]{:S(2)}) collective-permute-start(f32[4,4,1,256]{3,1,0,2:T(4,128)} %get-tuple-element.38), channel_id=1, source_target_pairs={{0,1},{1,2},{2,3},{3,4},{4,5},{5,6},{6,7},{8,9},{9,10},{10,11},{11... | collective-permute-start | bytes 49160 | tf_op jit(solution)/shard_map/ppermute | solution.py:45
  14.0 35.3 %collective-permute-start.3 = (f32[4,4,1,256]{3,1,0,2:T(4,128)}, f32[4,4,1,256]{3,1,0,2:T(4,128)}, u32[]{:S(2)}, u32[]{:S(2)}) collective-permute-start(f32[4,4,1,256]{3,1,0,2:T(4,128)} %get-tuple-element.39), channel_id=1, source_target_pairs={{1,0},{2,1},{3,2},{4,3},{5,4},{6,5},{7,6},{9,8},{10,9},{11,10},{12... | collective-permute-start | bytes 49160 | tf_op jit(solution)/shard_map/ppermute | solution.py:48
  22.7 26.7 %copy-start = (f32[4,4,64,256]{3,2,1,0:T(8,128)S(1)}, f32[4,4,64,256]{3,2,1,0:T(8,128)}, u32[]{:S(2)}) copy-start(f32[4,4,64,256]{3,2,1,0:T(8,128)} %param.12) | copy-start | bytes 3145732
  22.7 3.1 %copy-start.12 = (f32[1,1,4,4,256]{4,3,2,1,0:T(4,128)S(1)}, f32[1,1,4,4,256]{4,3,2,1,0:T(4,128)}, u32[]{:S(2)}) copy-start(f32[1,1,4,4,256]{4,3,2,1,0:T(4,128)} %bitcast_multiply_fusion.5) | copy-start | bytes 49156
  22.7 26.7 %copy-start.1 = (f32[4,4,64,255]{3,1,0,2:T(4,128)S(1)}, f32[4,4,64,255]{3,1,0,2:T(4,128)}, u32[]{:S(2)}) copy-start(f32[4,4,64,255]{3,1,0,2:T(4,128)} %get-tuple-element.45) | copy-start | bytes 3133444
  22.9 30.8 %copy-start.2 = (f32[4,64,256]{2,0,1:T(4,128)}, f32[4,64,256]{2,0,1:T(4,128)S(1)}, u32[]{:S(2)}) copy-start(f32[4,64,256]{2,0,1:T(4,128)S(1)} %copy.103) | copy-start | bytes 786436
  23.1 30.6 %copy-start.4 = (f32[4,64,256]{2,0,1:T(4,128)}, f32[4,64,256]{2,0,1:T(4,128)S(1)}, u32[]{:S(2)}) copy-start(f32[4,64,256]{2,0,1:T(4,128)S(1)} %copy.105) | copy-start | bytes 786436
  23.1 15.1 %collective-permute-start.2 = (f32[4,4,64,1]{3,1,0,2:T(4,128)}, f32[4,4,64,1]{3,1,0,2:T(4,128)S(1)}, u32[]{:S(2)}, u32[]{:S(2)}) collective-permute-start(f32[4,4,64,1]{3,1,0,2:T(4,128)} %get-tuple-element.42), channel_id=1, source_target_pairs={{0,8},{8,16},{16,24},{24,0},{1,9},{9,17},{17,25},{25,1},{2,10},{10... | collective-permute-start | bytes 12296 | tf_op jit(solution)/shard_map/ppermute | solution.py:45
  24.9 28.8 %copy-start.6 = (f32[4,64,256]{2,0,1:T(4,128)}, f32[4,64,256]{2,0,1:T(4,128)S(1)}, u32[]{:S(2)}) copy-start(f32[4,64,256]{2,0,1:T(4,128)S(1)} %copy.104) | copy-start | bytes 786436
  24.9 24.4 %collective-permute-start = (f32[4,4,64,1]{3,1,0,2:T(4,128)}, f32[4,4,64,1]{3,1,0,2:T(4,128)S(1)}, u32[]{:S(2)}, u32[]{:S(2)}) collective-permute-start(f32[4,4,64,1]{3,1,0,2:T(4,128)} %get-tuple-element.43), channel_id=1, source_target_pairs={{8,0},{16,8},{24,16},{0,24},{9,1},{17,9},{25,17},{1,25},{10,2},{18... | collective-permute-start | bytes 12296 | tf_op jit(solution)/shard_map/ppermute | solution.py:48
  25.8 28.0 %copy-start.8 = (f32[4,64,256]{2,0,1:T(4,128)}, f32[4,64,256]{2,0,1:T(4,128)S(1)}, u32[]{:S(2)}) copy-start(f32[4,64,256]{2,0,1:T(4,128)S(1)} %copy.106) | copy-start | bytes 786436
  26.6 27.2 %collective-permute-start.7 = (f32[2,4,4,256]{3,2,1,0:T(4,128)S(1)}, f32[2,4,4,256]{3,2,1,0:T(4,128)S(1)}, u32[]{:S(2)}, u32[]{:S(2)}) collective-permute-start(f32[2,4,4,256]{3,2,1,0:T(4,128)S(1)} %get-tuple-element.51), channel_id=1, source_target_pairs={{0,16},{8,24},{16,0},{24,8},{1,17},{9,25},{17,1},{25,9},{2,18},{10... | collective-permute-start | bytes 98312 | tf_op jit(solution)/shard_map/ppermute | solution.py:20
  53.7 4.7 %copy-start.13 = (f32[4]{0:T(128)S(1)}, f32[4]{0:T(128)}, u32[]{:S(2)}) copy-start(f32[4]{0:T(128)} %constant.80) | copy-start | bytes 52
  53.7 4.6 %copy-start.14 = (pred[256]{0:T(512)(128)(4,1)S(1)}, pred[256]{0:T(512)(128)(4,1)}, u32[]{:S(2)}) copy-start(pred[256]{0:T(512)(128)(4,1)} %compare_and_fusion) | copy-start | bytes 772
  59.7 33.0 %copy-start.3 = (f32[4,64,256]{2,0,1:T(4,128)S(1)}, f32[4,64,256]{2,0,1:T(4,128)}, u32[]{:S(2)}) copy-start(f32[4,64,256]{2,0,1:T(4,128)} %copy-done.2) | copy-start | bytes 786436
  59.7 33.0 %copy-start.5 = (f32[4,64,256]{2,0,1:T(4,128)S(1)}, f32[4,64,256]{2,0,1:T(4,128)}, u32[]{:S(2)}) copy-start(f32[4,64,256]{2,0,1:T(4,128)} %copy-done.4) | copy-start | bytes 786436
  59.7 33.0 %copy-start.7 = (f32[4,64,256]{2,0,1:T(4,128)S(1)}, f32[4,64,256]{2,0,1:T(4,128)}, u32[]{:S(2)}) copy-start(f32[4,64,256]{2,0,1:T(4,128)} %copy-done.6) | copy-start | bytes 786436
  59.7 33.0 %copy-start.9 = (f32[4,64,256]{2,0,1:T(4,128)S(1)}, f32[4,64,256]{2,0,1:T(4,128)}, u32[]{:S(2)}) copy-start(f32[4,64,256]{2,0,1:T(4,128)} %copy-done.8) | copy-start | bytes 786436
  60.4 8.2 %collective-permute-start.12 = (f32[1,4,4,256]{3,2,1,0:T(4,128)S(1)}, f32[1,4,4,256]{3,2,1,0:T(4,128)S(1)}, u32[]{:S(2)}, u32[]{:S(2)}) collective-permute-start(f32[1,4,4,256]{3,2,1,0:T(4,128)S(1)} %bitcast_multiply_fusion.1), channel_id=1, source_target_pairs={{0,8},{8,0},{16,24},{24,16},{1,9},{9,1},{17,25},{25,17},{2,10},{10... | collective-permute-start | bytes 49160 | tf_op jit(solution)/shard_map/ppermute | solution.py:20
  61.0 31.6 %collective-permute-start.11 = (f32[4,4,1,256]{3,1,0,2:T(4,128)S(1)}, f32[4,4,1,256]{3,1,0,2:T(4,128)S(1)}, u32[]{:S(2)}, u32[]{:S(2)}) collective-permute-start(f32[4,4,1,256]{3,1,0,2:T(4,128)S(1)} %get-tuple-element.30), channel_id=1, source_target_pairs={{0,1},{1,2},{2,3},{3,4},{4,5},{5,6},{6,7},{8,9},{9,10},{10,11},{11... | collective-permute-start | bytes 49160 | tf_op jit(solution)/shard_map/ppermute | solution.py:45
  63.0 29.7 %collective-permute-start.10 = (f32[4,4,1,256]{3,1,0,2:T(4,128)S(1)}, f32[4,4,1,256]{3,1,0,2:T(4,128)S(1)}, u32[]{:S(2)}, u32[]{:S(2)}) collective-permute-start(f32[4,4,1,256]{3,1,0,2:T(4,128)S(1)} %get-tuple-element.31), channel_id=1, source_target_pairs={{1,0},{2,1},{3,2},{4,3},{5,4},{6,5},{7,6},{9,8},{10,9},{11,10},{12... | collective-permute-start | bytes 49160 | tf_op jit(solution)/shard_map/ppermute | solution.py:48
  66.6 14.8 %collective-permute-start.9 = (f32[4,4,64,1]{3,1,0,2:T(4,128)S(1)}, f32[4,4,64,1]{3,1,0,2:T(4,128)S(1)}, u32[]{:S(2)}, u32[]{:S(2)}) collective-permute-start(f32[4,4,64,1]{3,1,0,2:T(4,128)S(1)} %get-tuple-element.34), channel_id=1, source_target_pairs={{0,8},{8,16},{16,24},{24,0},{1,9},{9,17},{17,25},{25,1},{2,10},{10... | collective-permute-start | bytes 12296 | tf_op jit(solution)/shard_map/ppermute | solution.py:45
  68.1 24.5 %collective-permute-start.8 = (f32[4,4,64,1]{3,1,0,2:T(4,128)S(1)}, f32[4,4,64,1]{3,1,0,2:T(4,128)S(1)}, u32[]{:S(2)}, u32[]{:S(2)}) collective-permute-start(f32[4,4,64,1]{3,1,0,2:T(4,128)S(1)} %get-tuple-element.35), channel_id=1, source_target_pairs={{8,0},{16,8},{24,16},{0,24},{9,1},{17,9},{25,17},{1,25},{10,2},{18... | collective-permute-start | bytes 12296 | tf_op jit(solution)/shard_map/ppermute | solution.py:48
  68.7 26.7 %collective-permute-start.13 = (f32[2,4,4,256]{3,2,1,0:T(4,128)S(1)}, f32[2,4,4,256]{3,2,1,0:T(4,128)S(1)}, u32[]{:S(2)}, u32[]{:S(2)}) collective-permute-start(f32[2,4,4,256]{3,2,1,0:T(4,128)S(1)} %get-tuple-element.49), channel_id=1, source_target_pairs={{0,16},{8,24},{16,0},{24,8},{1,17},{9,25},{17,1},{25,9},{2,18},{10... | collective-permute-start | bytes 98312 | tf_op jit(solution)/shard_map/ppermute | solution.py:20
